TPU v7x, 32 devices: a whole 2x2x4 slice. The times are simulated.
32 devices in a mesh: fiber: 16 (over z, y, core), freq: 2 (over x).
Axes of the slice: x: 2, y: 2, z: 4, core: 2. Of those that a mesh axis runs over, the one named last changes fastest.
Arguments:
- spectra: bfloat16 [2, 512, 16, 2048], P(None, 'freq', 'fiber'), may hold values from -128 to 128
- valid_mask: int32 [16, 2048], P('fiber'), may hold values 0 or 1
- pair_reach: int32 [16], replicated, may hold values from 1 to 2, as said below
Outputs:
- correlations: float32 [16, 5, 2, 128, 128], P('fiber', None, 'freq')
Inputs may be any that keep to these rules, and one draw needn't show every extreme that they name: Block b is paired with blocks b + 1 to b + pair_reach[b]; every draw holds some block with reach 1 and some with reach 2.
All inputs are finite; a program needn't handle non-finite values. No bound on the sum of `valid_mask` on one device may be relied on, other than what follows from the above.
Results may differ from a plain program's by a relative error of at most 0.0012.
Values may be sent and summed in bfloat16 or wider, within the bound.
A program may use at most 128 MiB of HBM per device.

v0:
```python
import functools

import jax
import jax.numpy as jnp
import numpy as np
from jax import lax
from jax.experimental import pallas as pl
from jax.experimental.pallas import tpu as pltpu
from jax.sharding import PartitionSpec as P

FREQS = 512
BAND = 2
LAG_DEV = 1


first_bin = 64.0
lag_step = 24.0
transform_length = 2048.0


def shifted(block, axis, distance):
    devices = range(lax.axis_size(axis))
    route = [(i - distance, i) for i in devices if i - distance in devices]
    return lax.ppermute(block, axis, route)


def twiddles(bins, lag_count):
    lag_values = jnp.arange(lag_count, dtype=jnp.float32) * lag_step
    angle = 2.0 * jnp.pi / transform_length * lag_values[:, None] * (first_bin + bins)[None, :]
    paired = jnp.stack([jnp.cos(angle), -jnp.sin(angle)], axis=2)
    return paired.reshape(lag_count, 2 * bins.shape[0])


def left_form(block_data):
    upper_half = jnp.concatenate([block_data[0], block_data[1]], axis=1)
    lower_half = jnp.concatenate([block_data[1], -block_data[0]], axis=1)
    return jnp.stack([upper_half, lower_half], axis=1)


def right_form(block_data):
    return jnp.concatenate([block_data[0], block_data[1]], axis=1)


def correlate(left_side, right_side, factors):
    products = jnp.einsum(
        "fkwi,fwj->fkij", left_side, right_side, preferred_element_type=jnp.float32
    )
    flattened = products.reshape(2 * products.shape[0], -1)
    return jnp.dot(factors, flattened, precision=lax.Precision.HIGHEST)


def select_entry(table, position):
    positions = jnp.arange(table.shape[0], dtype=jnp.int32)
    return jnp.sum(jnp.where(positions == position, table, 0))


def spectra_from(block_data, offset):
    return shifted(block_data, "fiber", offset)


def result_from(lag_tile, offset):
    return shifted(lag_tile, "fiber", offset)


def spread(spectra, valid_mask, pair_reach):
    groups = lax.axis_size("freq")
    fibers = lax.axis_size("fiber")
    lag_count = LAG_DEV * groups
    masked = spectra * valid_mask.astype(jnp.bfloat16)
    raw_blocks = lax.all_to_all(masked, "fiber", split_axis=3, concat_axis=2, tiled=True)
    values = raw_blocks.astype(jnp.float32)
    energy = (
        lax.psum(jnp.sum(values[0] * values[0] + values[1] * values[1], axis=0), "freq") / FREQS
    )
    resident = (values / jnp.sqrt(energy + 1e-06)).astype(jnp.bfloat16)
    location = lax.axis_index("fiber")
    bin_count = resident.shape[1]
    bins = lax.axis_index("freq") * bin_count + jnp.arange(bin_count, dtype=jnp.int32)
    factors = twiddles(bins.astype(jnp.float32), lag_count)
    block = resident.shape[3]
    own_left = left_form(resident)

    def nothing(left_side, right_side, table_part):
        return jnp.zeros((lag_count, block * block), jnp.float32)

    partials = []
    for offset in range(BAND + 1):
        other = resident if offset == 0 else spectra_from(resident, -offset)
        usable = jnp.logical_and(
            offset <= select_entry(pair_reach, location), location + offset < fibers
        )
        partials.append(lax.cond(usable, correlate, nothing, own_left, right_form(other), factors))
    summed = lax.psum_scatter(jnp.stack(partials), "freq", scatter_dimension=1, tiled=True)
    forward = [summed[0]]
    backward = []
    for offset in range(1, BAND + 1):
        forward.append(summed[offset])
        backward.append(result_from(summed[offset], offset))
    tiles = []
    for lag_tile in backward[::-1]:
        shaped = lag_tile.reshape(lag_tile.shape[0], block, block)
        tiles.append(jnp.swapaxes(shaped, 1, 2))
    for lag_tile in forward:
        tiles.append(lag_tile.reshape(lag_tile.shape[0], block, block))
    return jnp.stack(tiles)[None]


CORE_BIT = 0
MESH = pl.DeviceIdType.MESH


def fused_kernel(dims, reach_ref, x_ref, mask_ref, wave_ref, out_ref, white, acc, core_in, tile_in,
                 energy_buf, edge_out, edge_in, core_send, core_recv, tile_send, tile_recv,
                 energy_send, energy_recv, edge_send, edge_recv):
    fibers, groups, block, bins, freqs = dims
    lag_count = groups * LAG_DEV
    fbits = fibers.bit_length() - 1
    gbits = groups.bit_length() - 1
    channels = fibers * block
    offsets = BAND + 1
    me = lax.axis_index("fiber")
    group = lax.axis_index("freq")

    def bit_of(value, k):
        return lax.rem(lax.div(value, 1 << k), 2)

    def partner(axis, k):
        place = me if axis == "fiber" else group
        return {axis: place + (1 - 2 * bit_of(place, k)) * (1 << k)}

    fiber_axes = [("fiber", k) for k in range(1, fbits)]
    freq_axes = [("freq", k) for k in range(gbits)]
    orders = [
        freq_axes + fiber_axes,
        fiber_axes[:1] + fiber_axes[1:] + freq_axes,
        fiber_axes[1:] + freq_axes + fiber_axes[:1],
    ]
    steps = len(freq_axes) + len(fiber_axes)

    def mine(axis):
        return bit_of(me if axis[0] == "fiber" else group, axis[1])

    def tile_place(relative):
        b = bit_of(me, CORE_BIT)
        lag = 0
        for axis, r in relative.items():
            own = mine(axis)
            value = r * own + (1 - r) * (1 - own)
            if axis[0] == "fiber":
                b = b + value * (1 << axis[1])
            else:
                lag = lag + value * (1 << axis[1])
        return b, lag

    def tile_copy(p, s, slot, b, lag):
        axis = orders[p][s]
        return pltpu.make_async_remote_copy(
            src_ref=acc.at[b, p, lag],
            dst_ref=tile_in.at[p, s, slot],
            send_sem=tile_send.at[p, s, slot],
            recv_sem=tile_recv.at[p, s, slot],
            device_id=partner(*axis),
            device_id_type=MESH,
        )

    def slot_of(p, s, relative):
        slot = 0
        for axis in orders[p][s + 1:]:
            slot = slot * 2 + relative[axis]
        return slot

    barrier = pltpu.get_barrier_semaphore()
    hyper = [("fiber", k) for k in range(fbits)] + freq_axes
    for axis in hyper:
        pl.semaphore_signal(barrier, inc=1, device_id=partner(*axis), device_id_type=MESH)
    near = [d for o in range(1, offsets) for d in (o, -o)]

    def inside(d):
        return jnp.logical_and(me + d >= 0, me + d < fibers)

    for d in near:
        @pl.when(inside(d))
        def _():
            pl.semaphore_signal(barrier, inc=1, device_id={"fiber": me + d}, device_id_type=MESH)

    rows = 64
    chunks = 2 * bins // rows

    def add_energy(i, total):
        part = x_ref[pl.ds(pl.multiple_of(i * rows, rows), rows), :].astype(jnp.float32)
        return total + jnp.sum(part * part, axis=0, keepdims=True)

    energy = lax.fori_loop(0, chunks, add_energy, jnp.zeros((1, channels), jnp.float32))
    peers = len(hyper)
    for d in near:
        peers = peers + jnp.where(inside(d), 1, 0)
    pl.semaphore_wait(barrier, peers)

    for k in range(gbits):
        energy_buf[2 * k] = energy
        copy = pltpu.make_async_remote_copy(
            src_ref=energy_buf.at[2 * k],
            dst_ref=energy_buf.at[2 * k + 1],
            send_sem=energy_send.at[k],
            recv_sem=energy_recv.at[k],
            device_id=partner("freq", k),
            device_id_type=MESH,
        )
        copy.start()
        copy.wait()
        energy = energy + energy_buf[2 * k + 1]
    scale = mask_ref[...].astype(jnp.float32) / jnp.sqrt(energy * (1.0 / freqs) + 1e-06)

    def whiten(i, carry):
        at = pl.ds(pl.multiple_of(i * rows, rows), rows)
        white[at, pl.ds(0, channels)] = (x_ref[at, :].astype(jnp.float32) * scale).astype(jnp.bfloat16)
        return carry

    lax.fori_loop(0, chunks, whiten, 0)
    white[:, pl.ds(channels, BAND * block)] = jnp.zeros((2 * bins, BAND * block), jnp.bfloat16)

    first = pl.multiple_of(group * bins, bins)

    def block_tiles(b):
        start = pl.multiple_of(b * block, block)
        turned = white[:, pl.ds(start, block)].astype(jnp.float32).T
        upper, lower = turned[:, :bins], turned[:, bins:]
        right = white[:, pl.ds(start, offsets * block)]
        for lag in range(lag_count):
            c = wave_ref[pl.ds(lag, 1), pl.ds(first, bins)]
            s = wave_ref[pl.ds(lag_count + lag, 1), pl.ds(first, bins)]
            rotated = jnp.concatenate([c * upper - s * lower, s * upper + c * lower], axis=1)
            high = rotated.astype(jnp.bfloat16)
            low = (rotated - high.astype(jnp.float32)).astype(jnp.bfloat16)
            both = jnp.dot(
                jnp.concatenate([high, low], axis=0), right, preferred_element_type=jnp.float32
            )
            both = both[:block] + both[block:]
            for d in range(offsets):
                acc[b, d, lag] = both[:, d * block:(d + 1) * block]

    halves = fibers // 2
    core = bit_of(me, CORE_BIT)
    order_bits = [axis for axis in fiber_axes[1:2] + fiber_axes[:1] + fiber_axes[2:]]

    def relatives(j):
        found = {}
        for i, axis in enumerate(order_bits):
            found[axis] = bit_of(j, len(order_bits) - 1 - i)
        return found

    def core_copy(j, b):
        return pltpu.make_async_remote_copy(
            src_ref=acc.at[b],
            dst_ref=core_in.at[j],
            send_sem=core_send.at[j],
            recv_sem=core_recv.at[j],
            device_id=partner("fiber", CORE_BIT),
            device_id_type=MESH,
        )

    def other_half(j, carry):
        b, _ = tile_place(relatives(j))
        b = b + 1 - 2 * core
        block_tiles(b)
        core_copy(j, b).start()
        return carry

    def own_half(j, carry):
        relative = relatives(j)
        b, _ = tile_place(relative)
        block_tiles(b)
        core_copy(j, b).wait_recv()
        acc[b] = acc[b] + core_in[j]
        for p in range(offsets):
            lead = orders[p][0]
            for choice in range(1 << gbits):
                full = dict(relative)
                for i, axis in enumerate(freq_axes):
                    full[axis] = (choice >> i) & 1
                if lead in freq_axes:
                    if full[lead] == 0:
                        tile_copy(p, 0, slot_of(p, 0, full), *tile_place(full)).start()
                else:
                    @pl.when(full[lead] == 0)
                    def _():
                        tile_copy(p, 0, slot_of(p, 0, full), *tile_place(full)).start()
        return carry

    lax.fori_loop(0, halves, other_half, 0)
    lax.fori_loop(0, halves, own_half, 0)

    for s in range(steps):
        for slot in range(1 << (steps - 1 - s)):
            for p in range(offsets):
                relative = {axis: 1 for axis in orders[p][: s + 1]}
                rest = orders[p][s + 1:]
                for i, axis in enumerate(rest):
                    relative[axis] = (slot >> (len(rest) - 1 - i)) & 1
                b, lag = tile_place(relative)
                tile_copy(p, s, slot, b, lag).wait_recv()
                acc[b, p, lag] = acc[b, p, lag] + tile_in[p, s, slot]
                if rest and relative[rest[0]] == 0:
                    tile_copy(p, s + 1, slot_of(p, s + 1, relative), b, lag).start()

    reach = reach_ref[me]

    def edge_copy(d):
        return pltpu.make_async_remote_copy(
            src_ref=edge_out.at[d - 1],
            dst_ref=edge_in.at[d - 1],
            send_sem=edge_send.at[d - 1],
            recv_sem=edge_recv.at[d - 1],
            device_id={"fiber": me + d},
            device_id_type=MESH,
        )

    for d in range(1, offsets):
        usable = jnp.where(jnp.logical_and(d <= reach, me + d < fibers), 1.0, 0.0)
        tile = acc[me, d, group] * usable
        out_ref[BAND + d] = tile
        edge_out[d - 1] = tile.T

        @pl.when(inside(d))
        def _():
            edge_copy(d).start()
    out_ref[BAND] = acc[me, 0, group]

    for d in range(1, offsets):
        out_ref[BAND - d] = jnp.zeros((block, block), jnp.float32)

        @pl.when(inside(-d))
        def _():
            edge_copy(d).wait_recv()
            out_ref[BAND - d] = edge_in[d - 1]

    for d in range(1, offsets):
        @pl.when(inside(d))
        def _():
            edge_copy(d).wait_send()

    def drain(j, carry):
        b, _ = tile_place(relatives(j))
        core_copy(j, b + 1 - 2 * core).wait_send()
        return carry

    lax.fori_loop(0, halves, drain, 0)
    for s in range(steps):
        for slot in range(1 << (steps - 1 - s)):
            for p in range(offsets):
                tile_copy(p, s, slot, me, 0).wait_send()


def fused(spectra, valid_mask, pair_reach):
    groups, fibers = lax.axis_size("freq"), lax.axis_size("fiber")
    bins, channels = spectra.shape[1], spectra.shape[3]
    block = channels // fibers
    freqs = bins * groups
    lag_count = groups * LAG_DEV
    offsets = BAND + 1
    angle = (
        2.0 * np.pi / transform_length * lag_step
        * np.arange(lag_count)[:, None] * (first_bin + np.arange(freqs))[None, :]
    )
    wave = jnp.asarray(np.concatenate([np.cos(angle), np.sin(angle)]).astype(np.float32))
    steps = (groups.bit_length() - 1) + (fibers.bit_length() - 2)
    slots = 1 << (steps - 1)
    tile = (block, block)
    vmem = pl.BlockSpec(memory_space=pltpu.VMEM)
    sem = pltpu.SemaphoreType.DMA
    result = pl.pallas_call(
        functools.partial(fused_kernel, (fibers, groups, block, bins, freqs)),
        out_shape=jax.ShapeDtypeStruct((2 * BAND + 1,) + tile, jnp.float32),
        in_specs=[pl.BlockSpec(memory_space=pltpu.SMEM), vmem, vmem, vmem],
        out_specs=vmem,
        scratch_shapes=[
            pltpu.VMEM((2 * bins, channels + BAND * block), jnp.bfloat16),
            pltpu.VMEM((fibers, offsets, lag_count) + tile, jnp.float32),
            pltpu.VMEM((fibers // 2, offsets, lag_count) + tile, jnp.float32),
            pltpu.VMEM((offsets, steps, slots) + tile, jnp.float32),
            pltpu.VMEM((2 * (groups.bit_length() - 1), 1, channels), jnp.float32),
            pltpu.VMEM((BAND,) + tile, jnp.float32),
            pltpu.VMEM((BAND,) + tile, jnp.float32),
            sem((fibers // 2,)), sem((fibers // 2,)),
            sem((offsets, steps, slots)), sem((offsets, steps, slots)),
            sem((groups.bit_length() - 1,)), sem((groups.bit_length() - 1,)),
            sem((BAND,)), sem((BAND,)),
        ],
        compiler_params=pltpu.CompilerParams(
            collective_id=0, has_side_effects=True, vmem_limit_bytes=48 * 1024 * 1024
        ),
    )(pair_reach, spectra.reshape(2 * bins, channels), valid_mask, wave)
    return result[None, :, None]


def power_of_two(n):
    return n & (n - 1) == 0


def fits_on_chip(fibers, groups, spectra):
    block = spectra.shape[3] // fibers
    partial_bytes = 4 * fibers * (BAND + 1) * groups * LAG_DEV * block * block
    return (
        power_of_two(fibers) and power_of_two(groups) and fibers >= 8 and groups >= 2
        and block % 128 == 0 and spectra.shape[1] % 128 == 0 and partial_bytes <= 1 << 23
    )


def shards(spectra, valid_mask, pair_reach):
    if fits_on_chip(lax.axis_size("fiber"), lax.axis_size("freq"), spectra):
        return fused(spectra, valid_mask, pair_reach)
    return spread(spectra, valid_mask, pair_reach)


def solution(mesh):
    return jax.shard_map(
        shards,
        mesh=mesh,
        in_specs=(P(None, "freq", "fiber", None), P("fiber", None), P()),
        out_specs=P("fiber", None, "freq", None, None),
        check_vma=False,
    )
```

profile of v0, /device:TPU:0, one launch (start us, length us, event | category | flops | bytes accessed | tf_op | source)
XLA Modules:
  0.0 54.4 jit_solution(1462670357975569732)
XLA Ops:
  0.0 0.0 copy-start
  0.0 1.6 %copy-done = bf16[2,256,1,2048]{3,1,2,0:T(8,128)(2,1)S(1)} copy-done((bf16[2,256,1,2048]{3,1,2,0:T(8,128)(2,1)S(1)}, bf16[2,256,1,2048]{3,1,2,0:T(8,128)(2,1)}, u32[]{:S(2)}) %copy-start) | copy-done | bytes 2097176
  1.6 0.0 copy-start.1
  1.6 0.7 %copy-done.1 = s32[1,2048]{1,0:T(1,128)S(1)} copy-done((s32[1,2048]{1,0:T(1,128)S(1)}, s32[1,2048]{1,0:T(1,128)}, u32[]{:S(2)}) %copy-start.1) | copy-done | bytes 8216
  2.3 0.0 copy-start.2
  2.3 0.7 %copy-done.2 = f32[4,512]{1,0:T(4,128)S(1)} copy-done((f32[4,512]{1,0:T(4,128)S(1)}, f32[4,512]{1,0:T(4,128)}, u32[]{:S(2)}) %copy-start.2) | copy-done | bytes 8216
  3.0 0.0 copy-start.3
  3.0 0.7 %copy-done.3 = s32[16]{0:T(128)S(1)} copy-done((s32[16]{0:T(128)S(1)}, s32[16]{0:T(128)}, u32[]{:S(2)}) %copy-start.3) | copy-done | bytes 88
  3.6 50.0 %shard_map.46 = f32[5,128,128]{2,1,0:T(8,128)S(1)} custom-call(s32[16]{0:T(128)S(1)} %copy-done.3, bf16[512,2048]{1,0:T(8,128)(2,1)S(1)} %bitcast.4, s32[1,2048]{1,0:T(1,128)S(1)} %copy-done.1, f32[4,512]{1,0:T(4,128)S(1)} %copy-done.2), custom_call_target="tpu_custom_call" | custom-call | tf_op jit(solution)/shard_map/pallas_call | solution.py:371
  53.7 0.7 %copy.7 = f32[1,5,1,128,128]{4,3,2,1,0:T(8,128)} copy(f32[1,5,1,128,128]{4,3,2,1,0:T(8,128)S(1)} %bitcast.5) | data formatting | bytes 655360
Async XLA Ops:
  0.0 1.6 %copy-start = (bf16[2,256,1,2048]{3,1,2,0:T(8,128)(2,1)S(1)}, bf16[2,256,1,2048]{3,1,2,0:T(8,128)(2,1)}, u32[]{:S(2)}) copy-start(bf16[2,256,1,2048]{3,1,2,0:T(8,128)(2,1)} %param.4) | copy-start | bytes 6291460
  1.6 0.7 %copy-start.1 = (s32[1,2048]{1,0:T(1,128)S(1)}, s32[1,2048]{1,0:T(1,128)}, u32[]{:S(2)}) copy-start(s32[1,2048]{1,0:T(1,128)} %mask_ref.1) | copy-start | bytes 24580
  2.3 0.7 %copy-start.2 = (f32[4,512]{1,0:T(4,128)S(1)}, f32[4,512]{1,0:T(4,128)}, u32[]{:S(2)}) copy-start(f32[4,512]{1,0:T(4,128)} %constant.2.clone.wave_ref) | copy-start | bytes 24580
  3.0 0.7 %copy-start.3 = (s32[16]{0:T(128)S(1)}, s32[16]{0:T(128)}, u32[]{:S(2)}) copy-start(s32[16]{0:T(128)} %reach_ref.1) | copy-start | bytes 196
where the time goes:
time: 54.7 us; the launch traced here: 54.4 us
  Pallas kernels  50 us (91%)
  local copies, waits for them, and re-layouts  4.36 us (8%)
    pallas_call x1, Pallas kernels, fused(): pl.pallas_call(functools.partial(fused_kernel, (fibers, groups, block, bi...  50 us
    unnamed x9, local copies, waits for them, and re-layouts  4.36 us

commit v1 on v0

--- a/solution.py
+++ b/solution.py
@@ -130,11 +130,16 @@
 
     fiber_axes = [("fiber", k) for k in range(1, fbits)]
     freq_axes = [("freq", k) for k in range(gbits)]
+    near_axes, far_axes = fiber_axes[:1], fiber_axes[1:]
     orders = [
-        freq_axes + fiber_axes,
-        fiber_axes[:1] + fiber_axes[1:] + freq_axes,
-        fiber_axes[1:] + freq_axes + fiber_axes[:1],
+        freq_axes + near_axes + far_axes,
+        near_axes + freq_axes + far_axes,
+        freq_axes + far_axes + near_axes,
+        near_axes + far_axes + freq_axes,
     ]
+    orders = orders + orders[2:] * (offsets - 2)
+    portions = list(range(2, 2 * offsets)) + [0, 1]
+    half = block // 2
     steps = len(freq_axes) + len(fiber_axes)
 
     def mine(axis):
@@ -152,13 +157,20 @@
                 lag = lag + value * (1 << axis[1])
         return b, lag
 
+    def half_of(p):
+        return pl.ds((p % 2) * half, half)
+
+    def place_in(s, slot):
+        return (1 << steps) - (1 << (steps - s)) + slot
+
     def tile_copy(p, s, slot, b, lag):
         axis = orders[p][s]
+        place = place_in(s, slot)
         return pltpu.make_async_remote_copy(
-            src_ref=acc.at[b, p, lag],
-            dst_ref=tile_in.at[p, s, slot],
-            send_sem=tile_send.at[p, s, slot],
-            recv_sem=tile_recv.at[p, s, slot],
+            src_ref=acc.at[b, p // 2, lag, half_of(p)],
+            dst_ref=tile_in.at[p, place],
+            send_sem=tile_send.at[p, place],
+            recv_sem=tile_recv.at[p, place],
             device_id=partner(*axis),
             device_id_type=MESH,
         )
@@ -241,7 +253,7 @@
 
     halves = fibers // 2
     core = bit_of(me, CORE_BIT)
-    order_bits = [axis for axis in fiber_axes[1:2] + fiber_axes[:1] + fiber_axes[2:]]
+    order_bits = near_axes + far_axes
 
     def relatives(j):
         found = {}
@@ -259,20 +271,12 @@
             device_id_type=MESH,
         )
 
-    def other_half(j, carry):
-        b, _ = tile_place(relatives(j))
-        b = b + 1 - 2 * core
-        block_tiles(b)
-        core_copy(j, b).start()
-        return carry
-
-    def own_half(j, carry):
+    def finish(j):
         relative = relatives(j)
         b, _ = tile_place(relative)
-        block_tiles(b)
         core_copy(j, b).wait_recv()
         acc[b] = acc[b] + core_in[j]
-        for p in range(offsets):
+        for p in portions:
             lead = orders[p][0]
             for choice in range(1 << gbits):
                 full = dict(relative)
@@ -285,21 +289,34 @@
                     @pl.when(full[lead] == 0)
                     def _():
                         tile_copy(p, 0, slot_of(p, 0, full), *tile_place(full)).start()
+
+    def two_blocks(j, carry):
+        b, _ = tile_place(relatives(j))
+        other = b + 1 - 2 * core
+        block_tiles(other)
+        core_copy(j, other).start()
+
+        @pl.when(j > 0)
+        def _():
+            finish(j - 1)
+
+        block_tiles(b)
         return carry
 
-    lax.fori_loop(0, halves, other_half, 0)
-    lax.fori_loop(0, halves, own_half, 0)
+    lax.fori_loop(0, halves, two_blocks, 0)
+    finish(halves - 1)
 
     for s in range(steps):
         for slot in range(1 << (steps - 1 - s)):
-            for p in range(offsets):
+            for p in portions:
                 relative = {axis: 1 for axis in orders[p][: s + 1]}
                 rest = orders[p][s + 1:]
                 for i, axis in enumerate(rest):
                     relative[axis] = (slot >> (len(rest) - 1 - i)) & 1
                 b, lag = tile_place(relative)
                 tile_copy(p, s, slot, b, lag).wait_recv()
-                acc[b, p, lag] = acc[b, p, lag] + tile_in[p, s, slot]
+                part = acc[b, p // 2, lag, half_of(p)]
+                acc[b, p // 2, lag, half_of(p)] = part + tile_in[p, place_in(s, slot)]
                 if rest and relative[rest[0]] == 0:
                     tile_copy(p, s + 1, slot_of(p, s + 1, relative), b, lag).start()
 
@@ -347,7 +364,7 @@
     lax.fori_loop(0, halves, drain, 0)
     for s in range(steps):
         for slot in range(1 << (steps - 1 - s)):
-            for p in range(offsets):
+            for p in portions:
                 tile_copy(p, s, slot, me, 0).wait_send()
 
 
@@ -364,7 +381,7 @@
     )
     wave = jnp.asarray(np.concatenate([np.cos(angle), np.sin(angle)]).astype(np.float32))
     steps = (groups.bit_length() - 1) + (fibers.bit_length() - 2)
-    slots = 1 << (steps - 1)
+    slots = (1 << steps) - 1
     tile = (block, block)
     vmem = pl.BlockSpec(memory_space=pltpu.VMEM)
     sem = pltpu.SemaphoreType.DMA
@@ -377,12 +394,12 @@
             pltpu.VMEM((2 * bins, channels + BAND * block), jnp.bfloat16),
             pltpu.VMEM((fibers, offsets, lag_count) + tile, jnp.float32),
             pltpu.VMEM((fibers // 2, offsets, lag_count) + tile, jnp.float32),
-            pltpu.VMEM((offsets, steps, slots) + tile, jnp.float32),
+            pltpu.VMEM((2 * offsets, slots, block // 2, block), jnp.float32),
             pltpu.VMEM((2 * (groups.bit_length() - 1), 1, channels), jnp.float32),
             pltpu.VMEM((BAND,) + tile, jnp.float32),
             pltpu.VMEM((BAND,) + tile, jnp.float32),
             sem((fibers // 2,)), sem((fibers // 2,)),
-            sem((offsets, steps, slots)), sem((offsets, steps, slots)),
+            sem((2 * offsets, slots)), sem((2 * offsets, slots)),
             sem((groups.bit_length() - 1,)), sem((groups.bit_length() - 1,)),
             sem((BAND,)), sem((BAND,)),
         ],

time: 54.7 us -> 55 us (level)
  no operation moved by 1% of the time
where the time goes in v1:
time: 55 us; the launch traced here: 54.7 us
  Pallas kernels  50.4 us (92%)
  local copies, waits for them, and re-layouts  4.36 us (8%)
    pallas_call x1, Pallas kernels, fused(): pl.pallas_call(functools.partial(fused_kernel, (fibers, groups, block, bi...  50.4 us
    unnamed x9, local copies, waits for them, and re-layouts  4.36 us

profile of v1, /device:TPU:0, one launch (start us, length us, event | category | flops | bytes accessed | tf_op | source)
XLA Modules:
  0.0 54.7 jit_solution(7682506829994950391)
XLA Ops:
  0.0 0.0 copy-start
  0.0 1.6 %copy-done = bf16[2,256,1,2048]{3,1,2,0:T(8,128)(2,1)S(1)} copy-done((bf16[2,256,1,2048]{3,1,2,0:T(8,128)(2,1)S(1)}, bf16[2,256,1,2048]{3,1,2,0:T(8,128)(2,1)}, u32[]{:S(2)}) %copy-start) | copy-done | bytes 2097176
  1.6 0.0 copy-start.1
  1.6 0.7 %copy-done.1 = s32[1,2048]{1,0:T(1,128)S(1)} copy-done((s32[1,2048]{1,0:T(1,128)S(1)}, s32[1,2048]{1,0:T(1,128)}, u32[]{:S(2)}) %copy-start.1) | copy-done | bytes 8216
  2.3 0.0 copy-start.2
  2.3 0.7 %copy-done.2 = f32[4,512]{1,0:T(4,128)S(1)} copy-done((f32[4,512]{1,0:T(4,128)S(1)}, f32[4,512]{1,0:T(4,128)}, u32[]{:S(2)}) %copy-start.2) | copy-done | bytes 8216
  3.0 0.0 copy-start.3
  3.0 0.7 %copy-done.3 = s32[16]{0:T(128)S(1)} copy-done((s32[16]{0:T(128)S(1)}, s32[16]{0:T(128)}, u32[]{:S(2)}) %copy-start.3) | copy-done | bytes 88
  3.6 50.4 %shard_map.46 = f32[5,128,128]{2,1,0:T(8,128)S(1)} custom-call(s32[16]{0:T(128)S(1)} %copy-done.3, bf16[512,2048]{1,0:T(8,128)(2,1)S(1)} %bitcast.4, s32[1,2048]{1,0:T(1,128)S(1)} %copy-done.1, f32[4,512]{1,0:T(4,128)S(1)} %copy-done.2), custom_call_target="tpu_custom_call" | custom-call | tf_op jit(solution)/shard_map/pallas_call | solution.py:388
  54.0 0.7 %copy.7 = f32[1,5,1,128,128]{4,3,2,1,0:T(8,128)} copy(f32[1,5,1,128,128]{4,3,2,1,0:T(8,128)S(1)} %bitcast.5) | data formatting | bytes 655360
Async XLA Ops:
  0.0 1.6 %copy-start = (bf16[2,256,1,2048]{3,1,2,0:T(8,128)(2,1)S(1)}, bf16[2,256,1,2048]{3,1,2,0:T(8,128)(2,1)}, u32[]{:S(2)}) copy-start(bf16[2,256,1,2048]{3,1,2,0:T(8,128)(2,1)} %param.4) | copy-start | bytes 6291460
  1.6 0.7 %copy-start.1 = (s32[1,2048]{1,0:T(1,128)S(1)}, s32[1,2048]{1,0:T(1,128)}, u32[]{:S(2)}) copy-start(s32[1,2048]{1,0:T(1,128)} %mask_ref.1) | copy-start | bytes 24580
  2.3 0.7 %copy-start.2 = (f32[4,512]{1,0:T(4,128)S(1)}, f32[4,512]{1,0:T(4,128)}, u32[]{:S(2)}) copy-start(f32[4,512]{1,0:T(4,128)} %constant.2.clone.wave_ref) | copy-start | bytes 24580
  3.0 0.7 %copy-start.3 = (s32[16]{0:T(128)S(1)}, s32[16]{0:T(128)}, u32[]{:S(2)}) copy-start(s32[16]{0:T(128)} %reach_ref.1) | copy-start | bytes 196

commit v2 on v1

--- a/solution.py
+++ b/solution.py
@@ -106,10 +106,14 @@
 
 
 CORE_BIT = 0
+TURN, HOP = 2, 3
+LOAD_ROWS = 64
+PORTIONS = ("zxy", "zyx", "xyz", "yxz", "xyz", "yxz")
 MESH = pl.DeviceIdType.MESH
 
 
-def fused_kernel(dims, reach_ref, x_ref, mask_ref, wave_ref, out_ref, white, acc, core_in, tile_in,
+def fused_kernel(dims, reach_hbm, x_hbm, mask_hbm, wave_hbm, out_ref, reach_ref, x_ref, mask_ref, wave_ref,
+                 load_sem, small_sem, white, acc, core_in, tile_in,
                  energy_buf, edge_out, edge_in, core_send, core_recv, tile_send, tile_recv,
                  energy_send, energy_recv, edge_send, edge_recv):
     fibers, groups, block, bins, freqs = dims
@@ -131,14 +135,9 @@
     fiber_axes = [("fiber", k) for k in range(1, fbits)]
     freq_axes = [("freq", k) for k in range(gbits)]
     near_axes, far_axes = fiber_axes[:1], fiber_axes[1:]
-    orders = [
-        freq_axes + near_axes + far_axes,
-        near_axes + freq_axes + far_axes,
-        freq_axes + far_axes + near_axes,
-        near_axes + far_axes + freq_axes,
-    ]
-    orders = orders + orders[2:] * (offsets - 2)
-    portions = list(range(2, 2 * offsets)) + [0, 1]
+    named = {"x": freq_axes, "y": near_axes, "z": far_axes}
+    orders = [sum((named[n] for n in names), []) for names in PORTIONS]
+    portions = list(range(2 * offsets))
     half = block // 2
     steps = len(freq_axes) + len(fiber_axes)
 
@@ -181,6 +180,24 @@
             slot = slot * 2 + relative[axis]
         return slot
 
+    rows = LOAD_ROWS
+    chunks = 2 * bins // rows
+
+    def load(i):
+        at = pl.ds(pl.multiple_of(i * rows, rows), rows)
+        return pltpu.make_async_copy(x_hbm.at[at], x_ref.at[at], load_sem.at[i])
+
+    small = [
+        pltpu.make_async_copy(source, target, small_sem.at[i])
+        for i, (source, target) in enumerate(
+            [(mask_hbm, mask_ref), (wave_hbm, wave_ref), (reach_hbm, reach_ref)]
+        )
+    ]
+    for i in range(chunks):
+        load(i).start()
+    for copy in small:
+        copy.start()
+
     barrier = pltpu.get_barrier_semaphore()
     hyper = [("fiber", k) for k in range(fbits)] + freq_axes
     for axis in hyper:
@@ -195,10 +212,10 @@
         def _():
             pl.semaphore_signal(barrier, inc=1, device_id={"fiber": me + d}, device_id_type=MESH)
 
-    rows = 64
-    chunks = 2 * bins // rows
+    white[:, pl.ds(channels, BAND * block)] = jnp.zeros((2 * bins, BAND * block), jnp.bfloat16)
 
     def add_energy(i, total):
+        load(i).wait()
         part = x_ref[pl.ds(pl.multiple_of(i * rows, rows), rows), :].astype(jnp.float32)
         return total + jnp.sum(part * part, axis=0, keepdims=True)
 
@@ -208,6 +225,8 @@
         peers = peers + jnp.where(inside(d), 1, 0)
     pl.semaphore_wait(barrier, peers)
 
+    for copy in small:
+        copy.wait()
     for k in range(gbits):
         energy_buf[2 * k] = energy
         copy = pltpu.make_async_remote_copy(
@@ -229,7 +248,6 @@
         return carry
 
     lax.fori_loop(0, chunks, whiten, 0)
-    white[:, pl.ds(channels, BAND * block)] = jnp.zeros((2 * bins, BAND * block), jnp.bfloat16)
 
     first = pl.multiple_of(group * bins, bins)
 
@@ -306,19 +324,33 @@
     lax.fori_loop(0, halves, two_blocks, 0)
     finish(halves - 1)
 
+    def ready(p, s, relative):
+        if s < 0:
+            turn = 0
+            for axis in order_bits:
+                turn = 2 * turn + relative[axis]
+            return turn * TURN
+        axis = orders[p][s]
+        sent = ready(p, s - 1, {**relative, axis: 0}) + HOP
+        return max(sent, ready(p, s - 1, {**relative, axis: 1}))
+
+    events = []
     for s in range(steps):
         for slot in range(1 << (steps - 1 - s)):
             for p in portions:
+                rest = orders[p][s + 1:]
                 relative = {axis: 1 for axis in orders[p][: s + 1]}
-                rest = orders[p][s + 1:]
                 for i, axis in enumerate(rest):
                     relative[axis] = (slot >> (len(rest) - 1 - i)) & 1
-                b, lag = tile_place(relative)
-                tile_copy(p, s, slot, b, lag).wait_recv()
-                part = acc[b, p // 2, lag, half_of(p)]
-                acc[b, p // 2, lag, half_of(p)] = part + tile_in[p, place_in(s, slot)]
-                if rest and relative[rest[0]] == 0:
-                    tile_copy(p, s + 1, slot_of(p, s + 1, relative), b, lag).start()
+                events.append((ready(p, s, relative), s, len(events), p, slot, relative))
+    for _, s, _, p, slot, relative in sorted(events, key=lambda event: event[:3]):
+        rest = orders[p][s + 1:]
+        b, lag = tile_place(relative)
+        tile_copy(p, s, slot, b, lag).wait_recv()
+        part = acc[b, p // 2, lag, half_of(p)]
+        acc[b, p // 2, lag, half_of(p)] = part + tile_in[p, place_in(s, slot)]
+        if rest and relative[rest[0]] == 0:
+            tile_copy(p, s + 1, slot_of(p, s + 1, relative), b, lag).start()
 
     reach = reach_ref[me]
 
@@ -388,9 +420,14 @@
     result = pl.pallas_call(
         functools.partial(fused_kernel, (fibers, groups, block, bins, freqs)),
         out_shape=jax.ShapeDtypeStruct((2 * BAND + 1,) + tile, jnp.float32),
-        in_specs=[pl.BlockSpec(memory_space=pltpu.SMEM), vmem, vmem, vmem],
+        in_specs=[pl.BlockSpec(memory_space=pl.ANY)] * 4,
         out_specs=vmem,
         scratch_shapes=[
+            pltpu.SMEM(pair_reach.shape, jnp.int32),
+            pltpu.VMEM((2 * bins, channels), jnp.bfloat16),
+            pltpu.VMEM(valid_mask.shape, jnp.int32),
+            pltpu.VMEM(wave.shape, jnp.float32),
+            sem((2 * bins // LOAD_ROWS,)), sem((3,)),
             pltpu.VMEM((2 * bins, channels + BAND * block), jnp.bfloat16),
             pltpu.VMEM((fibers, offsets, lag_count) + tile, jnp.float32),
             pltpu.VMEM((fibers // 2, offsets, lag_count) + tile, jnp.float32),
@@ -404,7 +441,7 @@
             sem((BAND,)), sem((BAND,)),
         ],
         compiler_params=pltpu.CompilerParams(
-            collective_id=0, has_side_effects=True, vmem_limit_bytes=48 * 1024 * 1024
+            collective_id=0, has_side_effects=True, vmem_limit_bytes=60 * 1024 * 1024
         ),
     )(pair_reach, spectra.reshape(2 * bins, channels), valid_mask, wave)
     return result[None, :, None]

time: 55 us -> 49.4 us (0.90)
  the two profiles are of different devices: /device:TPU:0 before, /device:TPU:18 now
where the time goes in v2:
time: 49.4 us; the launch traced here: 49.3 us
  Pallas kernels  47.5 us (96%)
  local copies, waits for them, and re-layouts  1.72 us (3%)
    pallas_call x1, Pallas kernels, fused(): pl.pallas_call(functools.partial(fused_kernel, (fibers, groups, block, bi...  47.5 us
    unnamed x1, local copies, waits for them, and re-layouts  1.72 us

profile of v2, /device:TPU:18, one launch (start us, length us, event | category | flops | bytes accessed | tf_op | source)
XLA Modules:
  0.0 49.3 jit_solution(1794917349182610605)
XLA Ops:
  0.0 47.5 %shard_map.46 = f32[5,128,128]{2,1,0:T(8,128)} custom-call(s32[16]{0:T(128)} %reach_hbm.1, bf16[512,2048]{1,0:T(8,128)(2,1)} %bitcast.4, s32[1,2048]{1,0:T(1,128)} %mask_hbm.1, f32[4,512]{1,0:T(4,128)} %constant.2.clone.wave_hbm), custom_call_target="tpu_custom_call" | custom-call | tf_op jit(solution)/shard_map/pallas_call | solution.py:420
  47.5 1.7 %copy.7 = f32[1,5,1,128,128]{4,3,2,1,0:T(8,128)} copy(f32[1,5,1,128,128]{4,3,2,1,0:T(8,128)} %bitcast.5) | data formatting | bytes 655360

commit v3 on v2

--- a/solution.py
+++ b/solution.py
@@ -106,7 +106,7 @@
 
 
 CORE_BIT = 0
-TURN, HOP = 2, 3
+TURN, HOP = 2, 6
 LOAD_ROWS = 64
 PORTIONS = ("zxy", "zyx", "xyz", "yxz", "xyz", "yxz")
 MESH = pl.DeviceIdType.MESH

time: 49.4 us -> 48.2 us (0.976)
  the two profiles are of different devices: /device:TPU:18 before, /device:TPU:0 now
where the time goes in v3:
time: 48.2 us; the launch traced here: 47.4 us
  Pallas kernels  45.7 us (95%)
  local copies, waits for them, and re-layouts  1.72 us (4%)
    pallas_call x1, Pallas kernels, fused(): pl.pallas_call(functools.partial(fused_kernel, (fibers, groups, block, bi...  45.7 us
    unnamed x1, local copies, waits for them, and re-layouts  1.72 us

profile of v3, /device:TPU:0, one launch (start us, length us, event | category | flops | bytes accessed | tf_op | source)
XLA Modules:
  0.0 47.4 jit_solution(7225030362483408141)
XLA Ops:
  0.0 45.7 %shard_map.46 = f32[5,128,128]{2,1,0:T(8,128)} custom-call(s32[16]{0:T(128)} %reach_hbm.1, bf16[512,2048]{1,0:T(8,128)(2,1)} %bitcast.4, s32[1,2048]{1,0:T(1,128)} %mask_hbm.1, f32[4,512]{1,0:T(4,128)} %constant.2.clone.wave_hbm), custom_call_target="tpu_custom_call" | custom-call | tf_op jit(solution)/shard_map/pallas_call | solution.py:420
  45.7 1.7 %copy.7 = f32[1,5,1,128,128]{4,3,2,1,0:T(8,128)} copy(f32[1,5,1,128,128]{4,3,2,1,0:T(8,128)} %bitcast.5) | data formatting | bytes 655360
